TPU v7x, 512 devices: a whole 4x8x8 slice. The times are simulated.
512 devices in a mesh: space: 32 (over z, x), vel: 16 (over y, core).
Axes of the slice: x: 4, y: 8, z: 8, core: 2. Of those that a mesh axis runs over, the one named last changes fastest.
Arguments:
- dist: bfloat16 [512, 64, 4096], P('space', None, 'vel'), may hold values from -6 to 6
- send_faces: int32 [32, 2, 16], P('space'), may hold values from 0 to 95
- send_count: int32 [32, 2], P('space'), may hold values from 1 to 16, as said below
- source_face: int32 [512, 6], P('space'), may hold values from 0 to 127, as said below
- subface: int32 [512, 6], P('space'), may hold values from 0 to 4
- alpha: float32 [4, 4096], replicated, may hold values from -1 to 1
- beta: float32 [5, 4096], replicated, may hold values from -1 to 1
Outputs:
- relaxed: bfloat16 [512, 64, 4096], P('space', None, 'vel')
Inputs may be any that keep to these rules, and one draw needn't show every extreme that they name: `source_face`: for each face of a block: below 96 a local face of the same block; from 96 the 16 slots of the previous block's block toward the next one, then the 16 slots of the next block's block toward the previous one. Every slot of these two blocks is read by exactly one face of the block. `send_count`: for each direction some block's padded trace block is full. `send_faces`: local face numbers, element times 6 plus face.
All inputs are finite; a program needn't handle non-finite values.
Results may differ from a plain program's by a relative error of at most 0.0057.
Values may be sent and summed in bfloat16 or wider, within the bound.
No kernel may reach another device: no remote copies, remote signals or barrier semaphores. Data moves between devices by JAX's collectives and lax.ppermute only.
A program may use at most 64 MiB of HBM per device.

v0:
```python
import jax
import jax.numpy as jnp
import numpy as np
from jax import lax
from jax.sharding import PartitionSpec as P

VSIDE = 16
VEL = 4096
courant = 0.1
lift_weight = 6.0
relax_step = 0.5
highest = lax.Precision.HIGHEST


def passed_along(block, axis, distance):
    devices = range(lax.axis_size(axis))
    route = [((i - distance) % len(devices), i) for i in devices]
    return lax.ppermute(block, axis, route)


def shortened(array):

    def short(part):
        return part.astype(jnp.bfloat16) if part.dtype == jnp.float32 else part

    return jax.tree.map(short, array)


def lobatto_points():
    return np.array([-1.0, -1.0 / np.sqrt(5.0), 1.0 / np.sqrt(5.0), 1.0])


def lagrange_table(targets):
    points = lobatto_points()
    result = np.ones((targets.shape[0], 4))
    for column in range(4):
        for second in range(4):
            if second != column:
                result[:, column] = (
                    result[:, column]
                    * (targets - points[second])
                    / (points[column] - points[second])
                )
    return result


def derivative_table():
    points = lobatto_points()
    result = np.zeros((4, 4))
    for row_at in range(4):
        for column in range(4):
            total = 0.0
            for skipped in range(4):
                if skipped != column:
                    factor = 1.0 / (points[column] - points[skipped])
                    for second in range(4):
                        if second != column and second != skipped:
                            factor = (
                                factor
                                * (points[row_at] - points[second])
                                / (points[column] - points[second])
                            )
                    total = total + factor
            result[row_at, column] = total
    return result


def cosine_table():
    index_list = np.arange(VSIDE)
    result = np.sqrt(2.0 / VSIDE) * np.cos(
        np.pi * (index_list[None, :] + 0.5) * index_list[:, None] / VSIDE
    )
    result[0] = result[0] / np.sqrt(2.0)
    return result


def static_tables():
    derivative = derivative_table()
    eye_four = np.eye(4)
    gradients = np.stack(
        [
            np.kron(np.kron(derivative, eye_four), eye_four),
            np.kron(np.kron(eye_four, derivative), eye_four),
            np.kron(np.kron(eye_four, eye_four), derivative),
        ]
    )
    selector = np.zeros((96, 64))
    for axis_at in range(3):
        for side_at in range(2):
            filled = 0
            for node_at in range(64):
                digits = (node_at // 16, node_at // 4 % 4, node_at % 4)
                if digits[axis_at] == 3 * side_at:
                    selector[(2 * axis_at + side_at) * 16 + filled, node_at] = 1.0
                    filled = filled + 1
    points = lobatto_points()
    halves = [lagrange_table((points - 1.0) / 2.0), lagrange_table((points + 1.0) / 2.0)]
    mortar = np.stack(
        [np.eye(16)]
        + [np.kron(halves[(which - 1) // 2], halves[(which - 1) % 2]) for which in range(1, 5)]
    )
    return (gradients, selector, mortar)


def velocity_components(first, count):
    index_list = first + jnp.arange(count)
    along = [index_list // (VSIDE * VSIDE), index_list // VSIDE % VSIDE, index_list % VSIDE]
    return jnp.stack([(entry.astype(jnp.float32) + 0.5) * (2.0 / VSIDE) - 1.0 for entry in along])


def collide_element(element, kernels, cosine, cosine_pair):
    width = element.shape[0]
    kernel_rows = kernels.shape[0]
    modes = (kernel_rows - 1) // 2
    values = element.astype(jnp.float32)
    cube = values.reshape(width, VSIDE, VSIDE * VSIDE)
    inner = jnp.einsum("nir,qr->niq", cube, cosine_pair, precision=highest)
    spectrum = jnp.einsum("ai,niq->naq", cosine, inner, precision=highest).reshape(width, 1, VEL)
    filtered = (spectrum * kernels[None]).reshape(width * kernel_rows, VSIDE, VSIDE * VSIDE)
    outer = jnp.einsum("ai,naq->niq", cosine, filtered, precision=highest)
    fields = jnp.einsum("niq,qr->nir", outer, cosine_pair, precision=highest).reshape(
        width, kernel_rows, VEL
    )
    gain = jnp.sum(fields[:, :modes] * fields[:, modes : 2 * modes], axis=1)
    loss = values * fields[:, 2 * modes]
    return (values + relax_step * (gain - loss)).astype(jnp.bfloat16)


def on_device(dist, send_faces, send_count, source_face, subface, alpha, beta):
    elements = dist.shape[0]
    vel_local = dist.shape[2]
    slots = send_faces.shape[2]
    gradients, selector, mortar = static_tables()
    grad_low = jnp.asarray(gradients, jnp.bfloat16)
    select_low = jnp.asarray(selector, jnp.bfloat16)
    select_full = jnp.asarray(selector, jnp.float32)
    mortar_low = jnp.asarray(mortar, jnp.bfloat16)
    speeds = velocity_components(lax.axis_index("vel") * vel_local, vel_local)
    rows = (
        jnp.einsum("tn,env->etv", select_low, dist, preferred_element_type=jnp.float32)
        .astype(jnp.bfloat16)
        .reshape(elements * 6, 16, vel_local)
    )
    picked = rows[send_faces[0].reshape(-1)].reshape(2, slots, 16, vel_local)
    live = jnp.arange(slots)[None, :] < send_count[0][:, None]
    outgoing = jnp.where(live[:, :, None, None], picked, jnp.zeros_like(picked))
    from_prev = passed_along(outgoing[1], "space", 1)
    from_next = passed_along(outgoing[0], "space", -1)
    drift = jnp.zeros(dist.shape, jnp.float32)
    for axis_at in range(3):
        drift = drift + speeds[axis_at] * jnp.einsum(
            "nm,emv->env", grad_low[axis_at], dist, preferred_element_type=jnp.float32
        )
    table = jnp.concatenate([rows, from_prev, from_next], axis=0)
    neighbour = table[source_face.reshape(-1)]
    projected = jnp.einsum(
        "ftu,fuv->ftv",
        mortar_low[subface.reshape(-1)],
        neighbour,
        preferred_element_type=jnp.float32,
    )
    inflow = jnp.minimum(
        jnp.stack([-speeds[0], speeds[0], -speeds[1], speeds[1], -speeds[2], speeds[2]]), 0.0
    )
    jump = (rows.astype(jnp.float32) - projected).reshape(elements, 6, 16, vel_local) * inflow[
        None, :, None, :
    ]
    lifted = jnp.einsum(
        "tn,etv->env", select_full, jump.reshape(elements, 96, vel_local), precision=highest
    )
    updated = (dist.astype(jnp.float32) - courant * drift + courant * lift_weight * lifted).astype(
        jnp.bfloat16
    )
    cosine_np = cosine_table()
    cosine = jnp.asarray(cosine_np, jnp.float32)
    cosine_pair = jnp.asarray(np.kron(cosine_np, cosine_np), jnp.float32)
    kernels = jnp.concatenate([alpha, beta], axis=0)

    def one_element(element):
        return collide_element(element, kernels, cosine, cosine_pair)

    mixed = lax.map(
        one_element, lax.all_to_all(updated, "vel", split_axis=1, concat_axis=2, tiled=True)
    )
    relaxed = lax.all_to_all(
        shortened(mixed), "vel", split_axis=2, concat_axis=1, tiled=True
    ).astype(mixed.dtype)
    return relaxed


def solution(mesh):
    return jax.shard_map(
        on_device,
        mesh=mesh,
        in_specs=(
            P("space", None, "vel"),
            P("space", None, None),
            P("space", None),
            P("space", None),
            P("space", None),
            P(),
            P(),
        ),
        out_specs=P("space", None, "vel"),
        check_vma=False,
    )
```

profile of v0, /device:TPU:1, one launch (start us, length us, event | category | flops | bytes accessed | tf_op | source)
XLA Modules:
  0.0 151.0 jit_solution(12709845251339062603)
XLA Ops:
  0.0 0.8 reshape_squeeze.3
  0.8 0.7 iota_compare_fusion
  1.6 1.4 convolution_convert_fusion
  3.7 4.0 %collective-permute-start = (bf16[16,16,256]{2,1,0:T(8,128)(2,1)S(1)}, bf16[16,16,256]{2,1,0:T(8,128)(2,1)S(1)}, u32[]{:S(2)}, u32[]{:S(2)}) collective-permute-start(bf16[16,16,256]{2,1,0:T(8,128)(2,1)S(1)} %get-tuple-element.63), channel_id=1, source_target_pairs={{496,0},{0,16},{16,32},{32,48},{48,64},{64,80},{80,96},{96,112},{1... | collective-permute-start | bytes 393224 | tf_op jit(solution)/shard_map/ppermute | solution.py:18
  7.7 11.7 %collective-permute-start.1 = (bf16[16,16,256]{2,1,0:T(8,128)(2,1)S(1)}, bf16[16,16,256]{2,1,0:T(8,128)(2,1)}, u32[]{:S(2)}, u32[]{:S(2)}) collective-permute-start(bf16[16,16,256]{2,1,0:T(8,128)(2,1)S(1)} %get-tuple-element.64), channel_id=1, source_target_pairs={{16,0},{32,16},{48,32},{64,48},{80,64},{96,80},{112,96},{128,112},... | collective-permute-start | bytes 393224 | tf_op jit(solution)/shard_map/ppermute | solution.py:18
  21.3 0.7 gather_fusion
  22.0 1.0 pad_maximum_fusion
  23.1 1.5 %gather_fusion.2 = bf16[96,16,256]{2,1,0:T(8,128)(2,1)} fusion(bf16[128,16,256]{2,1,0:T(8,128)(2,1)S(1)} %pad_maximum_fusion, s32[1024]{0:T(1024)S(1)} %pad_clamp_fusion), kind=kCustom, calls=%fused_computation.2 | custom fusion | bytes 1573248 | tf_op jit(solution)/shard_map/gather | solution.py:155
  24.6 1.5 convert_subtract_fusion
  26.9 1.2 fusion.13
  28.1 1.1 copy.25
  29.2 8.1 %all-to-all-start = ((bf16[16,64,256]{2,0,1:T(8,128)(2,1)}), bf16[16,64,256]{2,0,1:T(8,128)(2,1)S(1)}, u32[]{:S(2)}, u32[]{:S(2)}) async-start(bf16[16,64,256]{2,0,1:T(8,128)(2,1)} %copy.25), calls=%async_computation | async-start | bytes 1048576 | tf_op jit(solution)/shard_map/all_to_all | solution.py:183
  37.4 17.2 %all-to-all-done = bf16[16,64,256]{2,0,1:T(8,128)(2,1)S(1)} async-done(((bf16[16,64,256]{2,0,1:T(8,128)(2,1)}), bf16[16,64,256]{2,0,1:T(8,128)(2,1)S(1)}, u32[]{:S(2)}, u32[]{:S(2)}) %all-to-all-start) | async-done | bytes 524320 | tf_op jit(solution)/shard_map/all_to_all | solution.py:183
  54.7 54.8 %while.11 = (s32[]{:T(128)}, bf16[16,4,4096]{2,0,1:T(8,128)(2,1)S(1)}, bf16[16,4,4096]{2,0,1:T(8,128)(2,1)S(1)}, f32[9,4096]{1,0:T(8,128)S(1)}, s32[]{:T(128)}, ...) while((s32[]{:T(128)}, bf16[16,4,4096]{2,0,1:T(8,128)(2,1)S(1)}, ...), condition=%wide.region_2.3_spmd.clone, body=%wide.region_0.2_spmd.sunk.clone.sunk | while | flops 535134208 | bytes 7325801 | solution.py:182
  55.7 0.7 convolution_bitcast_fusion.5
  57.5 0.7 dynamic_update_slice.7
  59.1 0.7 convolution_bitcast_fusion.5
  60.9 0.7 dynamic_update_slice.7
  62.6 0.7 convolution_bitcast_fusion.5
  64.3 0.7 dynamic_update_slice.7
  66.0 0.7 convolution_bitcast_fusion.5
  67.8 0.7 dynamic_update_slice.7
  69.4 0.7 convolution_bitcast_fusion.5
  71.2 0.7 dynamic_update_slice.7
  72.8 0.7 convolution_bitcast_fusion.5
  74.6 0.7 dynamic_update_slice.7
  76.3 0.7 convolution_bitcast_fusion.5
  78.1 0.7 dynamic_update_slice.7
  79.7 0.7 convolution_bitcast_fusion.5
  81.5 0.7 dynamic_update_slice.7
  84.9 0.7 dynamic_update_slice.7
  86.5 0.7 convolution_bitcast_fusion.5
  88.3 0.7 dynamic_update_slice.7
  91.8 0.7 dynamic_update_slice.7
  93.4 0.7 convolution_bitcast_fusion.5
  95.2 0.7 dynamic_update_slice.7
  98.6 0.7 dynamic_update_slice.7
  100.3 0.7 convolution_bitcast_fusion.5
  102.1 0.7 dynamic_update_slice.7
  105.5 0.7 dynamic_update_slice.7
  107.1 0.7 convolution_bitcast_fusion.5
  108.9 0.7 dynamic_update_slice.7
  109.6 4.6 %copy.27 = bf16[16,4,4096]{0,1,2:T(4,128)(2,1)} copy(bf16[16,4,4096]{2,0,1:T(8,128)(2,1)S(1)} %get-tuple-element.37) | data formatting | bytes 1048576 | tf_op jit(solution)/shard_map/while | solution.py:182
  114.2 5.7 %reshape.472 = bf16[16,2,8192]{2,1,0:T(2,128)(2,1)S(1)} reshape(bf16[4096,4,16]{2,1,0:T(4,128)(2,1)} %bitcast.110) | data formatting | bytes 1048576
  119.9 20.0 %all_to_all.36 = bf16[16,2,8192]{2,1,0:T(2,128)(2,1)S(1)} all-to-all(bf16[16,2,8192]{2,1,0:T(2,128)(2,1)S(1)} %reshape.472), channel_id=1, replica_groups=mesh['space'=32,'vel'=16] {'vel'}, dimensions={0} | all-to-all | bytes 1048576 | tf_op jit(solution)/shard_map/all_to_all | solution.py:185
  139.9 4.1 %reshape.473 = bf16[4096,4,16]{2,1,0:T(4,128)(2,1)} reshape(bf16[16,2,8192]{2,1,0:T(2,128)(2,1)S(1)} %all_to_all.36) | data formatting | bytes 1048576
  144.1 6.0 %copy.28 = bf16[16,16,4,256]{3,2,1,0:T(4,128)(2,1)S(1)} copy(bf16[16,16,4,256]{0,2,3,1:T(4,128)(2,1)} %bitcast.111) | data formatting | bytes 1048576 | tf_op jit(solution)/shard_map/all_to_all | solution.py:185
  150.1 0.9 all_to_all.33
  (218 shorter events, 38.0 us)
Async XLA Ops:
  0.0 19.9 %copy-start.9 = (bf16[64,64,1]{1,0,2:T(8,128)(2,1)S(1)}, bf16[64,64,1]{1,0,2:T(8,128)(2,1)}, u32[]{:S(2)}) copy-start(bf16[64,64,1]{1,0,2:T(8,128)(2,1)} %constant.122) | copy-start | bytes 24580
  0.0 20.0 %copy-start.1 = (bf16[16,64,256]{2,1,0:T(8,128)(2,1)S(1)}, bf16[16,64,256]{2,1,0:T(8,128)(2,1)}, u32[]{:S(2)}) copy-start(bf16[16,64,256]{2,1,0:T(8,128)(2,1)} %param.15) | copy-start | bytes 1572868
  0.0 19.5 %copy-start.10 = (s32[16,6]{0,1:T(8,128)S(1)}, s32[16,6]{0,1:T(8,128)}, u32[]{:S(2)}) copy-start(s32[16,6]{0,1:T(8,128)} %param.18) | copy-start | bytes 1156
  0.0 19.7 %copy-start.11 = (s32[16,6]{0,1:T(8,128)S(1)}, s32[16,6]{0,1:T(8,128)}, u32[]{:S(2)}) copy-start(s32[16,6]{0,1:T(8,128)} %param.19) | copy-start | bytes 1156
  3.0 17.3 %copy-start.8 = (bf16[64,64,1]{1,0,2:T(8,128)(2,1)S(1)}, bf16[64,64,1]{1,0,2:T(8,128)(2,1)}, u32[]{:S(2)}) copy-start(bf16[64,64,1]{1,0,2:T(8,128)(2,1)} %constant.123) | copy-start | bytes 24580
  3.7 18.3 %collective-permute-start = (bf16[16,16,256]{2,1,0:T(8,128)(2,1)S(1)}, bf16[16,16,256]{2,1,0:T(8,128)(2,1)S(1)}, u32[]{:S(2)}, u32[]{:S(2)}) collective-permute-start(bf16[16,16,256]{2,1,0:T(8,128)(2,1)S(1)} %get-tuple-element.63), channel_id=1, source_target_pairs={{496,0},{0,16},{16,32},{32,48},{48,64},{64,80},{80,96},{96,112},{1... | collective-permute-start | bytes 393224 | tf_op jit(solution)/shard_map/ppermute | solution.py:18
  7.7 14.3 %collective-permute-start.1 = (bf16[16,16,256]{2,1,0:T(8,128)(2,1)S(1)}, bf16[16,16,256]{2,1,0:T(8,128)(2,1)}, u32[]{:S(2)}, u32[]{:S(2)}) collective-permute-start(bf16[16,16,256]{2,1,0:T(8,128)(2,1)S(1)} %get-tuple-element.64), channel_id=1, source_target_pairs={{16,0},{32,16},{48,32},{64,48},{80,64},{96,80},{112,96},{128,112},... | collective-permute-start | bytes 393224 | tf_op jit(solution)/shard_map/ppermute | solution.py:18
  20.3 0.7 copy-start.7
  20.6 0.7 copy-start.2
  26.1 0.8 copy-start.6
  28.1 9.3 %copy-start.4 = (f32[5,4096]{1,0:T(8,128)S(1)}, f32[5,4096]{1,0:T(8,128)}, u32[]{:S(2)}) copy-start(f32[5,4096]{1,0:T(8,128)} %param.21) | copy-start | bytes 245764
  28.1 9.3 %copy-start.5 = (f32[4,4096]{1,0:T(4,128)S(1)}, f32[4,4096]{1,0:T(4,128)}, u32[]{:S(2)}) copy-start(f32[4,4096]{1,0:T(4,128)} %param.20) | copy-start | bytes 196612
  28.1 26.6 %copy-start = (f32[256,256,1]{1,0,2:T(8,128)S(1)}, f32[256,256,1]{1,0,2:T(8,128)}, u32[]{:S(2)}) copy-start(f32[256,256,1]{1,0,2:T(8,128)} %constant.232) | copy-start | bytes 786436
  28.1 26.6 %copy-start.3 = (f32[16,16,1]{1,0,2:T(8,128)S(1)}, f32[16,16,1]{1,0,2:T(8,128)}, u32[]{:S(2)}) copy-start(f32[16,16,1]{1,0,2:T(8,128)} %constant.233) | copy-start | bytes 3076
  29.2 25.5 %all-to-all-start = ((bf16[16,64,256]{2,0,1:T(8,128)(2,1)}), bf16[16,64,256]{2,0,1:T(8,128)(2,1)S(1)}, u32[]{:S(2)}, u32[]{:S(2)}) async-start(bf16[16,64,256]{2,0,1:T(8,128)(2,1)} %copy.25), calls=%async_computation | async-start | bytes 1048576 | tf_op jit(solution)/shard_map/all_to_all | solution.py:183
where the time goes:
time: 152 us; the launch traced here: 151 us
  local copies, waits for them, and re-layouts  45.7 us (30%)
  matrix products  33.2 us (22%)
  starting transfers between devices  23.8 us (16%)
  blocking collectives  20 us (13%)
  waiting for transfers between devices  17.3 us (11%)
  other arithmetic  9.18 us (6%)
  loops' own time  1.55 us (1%)
    all_to_all x1, blocking collectives, on_device(): lax.all_to_all(shortened(mixed), 'vel', split_axis=2, concat_axis=1, tile...  20 us
    all_to_all x1, waiting for transfers between devices, on_device(): lax.all_to_all(updated, 'vel', split_axis=1, concat_axis=2, tiled=True)  17.2 us
    ppermute x2, starting transfers between devices, passed_along(): return lax.ppermute(block, axis, route)  15.6 us
    unnamed x28, local copies, waits for them, and re-layouts  11.1 us
    dynamic_update_slice x16, local copies, waits for them, and re-layouts, on_device(): lax.map(one_element, lax.all_to_all(updated, 'vel', split_axis=1, concat_...  10.7 us
    dot_general x16, matrix products, collide_element(): outer = jnp.einsum('ai,naq->niq', cosine, filtered, precision=highest)  10.6 us
    dot_general x16, matrix products, collide_element(): jnp.einsum('niq,qr->nir', outer, cosine_pair, precision=highest)  10.1 us
    all_to_all x1, starting transfers between devices, on_device(): lax.all_to_all(updated, 'vel', split_axis=1, concat_axis=2, tiled=True)  8.15 us
  transfers between devices with their start and end apart: 3, of which 1 were waited for; matrix products, arithmetic and copies ran while one was open for 1% of the time, Pallas kernels for 0%

commit v1 on v0

--- a/solution.py
+++ b/solution.py
@@ -10,6 +10,13 @@
 lift_weight = 6.0
 relax_step = 0.5
 highest = lax.Precision.HIGHEST
+
+
+def swap_blocks(block, mesh_axis, split, join):
+    size = lax.axis_size(mesh_axis)
+    blocks = jnp.stack(jnp.split(block, size, axis=split), axis=0)
+    blocks = lax.all_to_all(blocks, mesh_axis, split_axis=0, concat_axis=0)
+    return jnp.concatenate(blocks, axis=join)
 
 
 def passed_along(block, axis, distance):
@@ -182,9 +189,7 @@
     mixed = lax.map(
         one_element, lax.all_to_all(updated, "vel", split_axis=1, concat_axis=2, tiled=True)
     )
-    relaxed = lax.all_to_all(
-        shortened(mixed), "vel", split_axis=2, concat_axis=1, tiled=True
-    ).astype(mixed.dtype)
+    relaxed = swap_blocks(shortened(mixed), "vel", 2, 1).astype(mixed.dtype)
     return relaxed
 
 

time: 152 us -> 133 us (0.88)
  local copies, waits for them, and re-layouts: 45.7 us -> 26.7 us
    unnamed x28 -> x45, local copies, waits for them, and re-layouts: 11.1 us -> 2.01 us
    all_to_all x2 -> x0, local copies, waits for them, and re-layouts: 6.95 us -> none  [on_device(): lax.all_to_all(shortened(mixed), 'vel', split_axis=2, concat_axis=1, tile...]
    while x17 -> x16, local copies, waits for them, and re-layouts: 5.33 us -> 0.73 us  [the longest x1 4.6 us: on_device(): lax.map(one_element, lax.all_to_all(updated, 'vel', split_axis=1, concat_...]
  transfers between devices with their start and end apart: 3 -> 3, of which waited for: 1 -> 1; matrix products, arithmetic and copies ran while one was open for 1% -> 2% of each run, Pallas kernels for 0% -> 0%
where the time goes in v1:
time: 133 us; the launch traced here: 132 us
  matrix products  33.3 us (25%)
  local copies, waits for them, and re-layouts  26.7 us (20%)
  starting transfers between devices  23.7 us (18%)
  blocking collectives  20 us (15%)
  waiting for transfers between devices  17.3 us (13%)
  other arithmetic  9.46 us (7%)
  loops' own time  1.42 us (1%)
    all_to_all x1, blocking collectives, swap_blocks(): blocks = lax.all_to_all(blocks, mesh_axis, split_axis=0, concat_axis=0)  20 us
    all_to_all x1, waiting for transfers between devices, on_device(): lax.all_to_all(updated, 'vel', split_axis=1, concat_axis=2, tiled=True)  17.2 us
    ppermute x2, starting transfers between devices, passed_along(): return lax.ppermute(block, axis, route)  15.6 us
    dynamic_update_slice x16, local copies, waits for them, and re-layouts, on_device(): lax.map(one_element, lax.all_to_all(updated, 'vel', split_axis=1, concat_...  10.7 us
    dot_general x16, matrix products, collide_element(): outer = jnp.einsum('ai,naq->niq', cosine, filtered, precision=highest)  10.6 us
    dot_general x16, matrix products, collide_element(): jnp.einsum('niq,qr->nir', outer, cosine_pair, precision=highest)  10.1 us
    all_to_all x1, starting transfers between devices, on_device(): lax.all_to_all(updated, 'vel', split_axis=1, concat_axis=2, tiled=True)  8.08 us
    dot_general x16, matrix products, collide_element(): inner = jnp.einsum('nir,qr->niq', cube, cosine_pair, precision=highest)  4.44 us
  transfers between devices with their start and end apart: 3, of which 1 were waited for; matrix products, arithmetic and copies ran while one was open for 2% of the time, Pallas kernels for 0%

profile of v1, /device:TPU:1, one launch (start us, length us, event | category | flops | bytes accessed | tf_op | source)
XLA Modules:
  0.0 132.3 jit_solution(8693689604470559746)
XLA Ops:
  0.0 0.8 reshape_squeeze.3
  0.8 0.7 iota_compare_fusion
  1.5 1.5 %convolution_convert_fusion = bf16[96,16,256]{2,0,1:T(8,128)(2,1)S(1)} fusion(bf16[96,64,1]{0,1,2:T(8,128)(2,1)} %constant.125, bf16[16,64,256]{2,1,0:T(8,128)(2,1)} %param.15), kind=kOutput, calls=%fused_computation.18 | convolution fusion | flops 50724864 | bytes 1323008 | tf_op jit(solution)/shard_map/tn,env->etv/dot_general | solution.py:147
  3.8 3.9 %collective-permute-start = (bf16[16,16,256]{2,1,0:T(8,128)(2,1)S(1)}, bf16[16,16,256]{2,1,0:T(8,128)(2,1)S(1)}, u32[]{:S(2)}, u32[]{:S(2)}) collective-permute-start(bf16[16,16,256]{2,1,0:T(8,128)(2,1)S(1)} %get-tuple-element.63), channel_id=1, source_target_pairs={{496,0},{0,16},{16,32},{32,48},{48,64},{64,80},{80,96},{96,112},{1... | collective-permute-start | bytes 393224 | tf_op jit(solution)/shard_map/ppermute | solution.py:25
  7.7 11.7 %collective-permute-start.1 = (bf16[16,16,256]{2,1,0:T(8,128)(2,1)S(1)}, bf16[16,16,256]{2,1,0:T(8,128)(2,1)}, u32[]{:S(2)}, u32[]{:S(2)}) collective-permute-start(bf16[16,16,256]{2,1,0:T(8,128)(2,1)S(1)} %get-tuple-element.64), channel_id=1, source_target_pairs={{16,0},{32,16},{48,32},{64,48},{80,64},{96,80},{112,96},{128,112},... | collective-permute-start | bytes 393224 | tf_op jit(solution)/shard_map/ppermute | solution.py:25
  19.9 1.4 %gather_fusion = bf16[96,16,16]{2,1,0:T(8,128)(2,1)} fusion(bf16[5,16,16]{2,1,0:T(8,128)(2,1)S(1)} %copy-done.2, s32[1024]{0:T(1024)S(1)} %get-tuple-element.74), kind=kCustom, calls=%fused_computation | custom fusion | bytes 98688 | tf_op jit(solution)/shard_map/gather | solution.py:165
  23.4 1.1 pad_maximum_fusion
  24.5 1.5 %gather_fusion.2 = bf16[96,16,256]{2,1,0:T(8,128)(2,1)} fusion(bf16[128,16,256]{2,1,0:T(8,128)(2,1)S(1)} %pad_maximum_fusion, s32[1024]{0:T(1024)S(1)} %get-tuple-element.73), kind=kCustom, calls=%fused_computation.2 | custom fusion | bytes 1573248 | tf_op jit(solution)/shard_map/gather | solution.py:162
  26.0 1.5 %convert_subtract_fusion = f32[96,16,256]{2,1,0:T(8,128)S(1)} fusion(bf16[96,16,256]{2,1,0:T(8,128)(2,1)S(1)} %bitcast.142, bf16[96,16,16]{2,1,0:T(8,128)(2,1)S(1)} %copy-done.3, bf16[96,16,256]{2,1,0:T(8,128)(2,1)} %gather_fusion.2), kind=kOutput, calls=%fused_computation.17 | convolution fusion | flops 13369344 | bytes 3194880 | tf_op jit(solution)/shard_map/ftu,fuv->ftv/dot_general | solution.py:163
  28.3 1.3 fusion.13
  29.6 1.1 copy.25
  30.7 8.1 %all-to-all-start = ((bf16[16,64,256]{2,0,1:T(8,128)(2,1)}), bf16[16,64,256]{2,0,1:T(8,128)(2,1)S(1)}, u32[]{:S(2)}, u32[]{:S(2)}) async-start(bf16[16,64,256]{2,0,1:T(8,128)(2,1)} %copy.25), calls=%async_computation | async-start | bytes 1048576 | tf_op jit(solution)/shard_map/all_to_all | solution.py:190
  38.8 17.2 %all-to-all-done = bf16[16,64,256]{2,0,1:T(8,128)(2,1)S(1)} async-done(((bf16[16,64,256]{2,0,1:T(8,128)(2,1)}), bf16[16,64,256]{2,0,1:T(8,128)(2,1)S(1)}, u32[]{:S(2)}, u32[]{:S(2)}) %all-to-all-start) | async-done | bytes 524320 | tf_op jit(solution)/shard_map/all_to_all | solution.py:190
  56.1 55.0 %while.11 = (s32[]{:T(128)}, bf16[16,4,4096]{2,0,1:T(8,128)(2,1)S(1)}, bf16[16,4,4096]{2,0,1:T(8,128)(2,1)S(1)}, f32[9,4096]{1,0:T(8,128)S(1)}, s32[]{:T(128)}, ...) while((s32[]{:T(128)}, bf16[16,4,4096]{2,0,1:T(8,128)(2,1)S(1)}, ...), condition=%wide.region_2.3_spmd.clone, body=%wide.region_0.2_spmd.sunk.clone.sunk | while | flops 535134208 | bytes 7325793 | solution.py:189
  57.1 0.7 convolution_bitcast_fusion.5
  58.9 0.7 dynamic_update_slice.7
  60.5 0.7 convolution_bitcast_fusion.5
  62.3 0.7 dynamic_update_slice.7
  64.0 0.7 convolution_bitcast_fusion.5
  65.7 0.7 dynamic_update_slice.7
  67.4 0.7 convolution_bitcast_fusion.5
  69.2 0.7 dynamic_update_slice.7
  70.8 0.7 convolution_bitcast_fusion.5
  72.6 0.7 dynamic_update_slice.7
  74.3 0.7 convolution_bitcast_fusion.5
  76.1 0.7 dynamic_update_slice.7
  77.7 0.7 convolution_bitcast_fusion.5
  79.5 0.7 dynamic_update_slice.7
  81.1 0.7 convolution_bitcast_fusion.5
  82.9 0.7 dynamic_update_slice.7
  84.6 0.7 convolution_bitcast_fusion.5
  86.4 0.7 dynamic_update_slice.7
  88.0 0.7 convolution_bitcast_fusion.5
  89.8 0.7 dynamic_update_slice.7
  91.4 0.7 convolution_bitcast_fusion.5
  93.2 0.7 dynamic_update_slice.7
  94.9 0.7 convolution_bitcast_fusion.5
  96.7 0.7 dynamic_update_slice.7
  98.3 0.7 convolution_bitcast_fusion.5
  100.1 0.7 dynamic_update_slice.7
  101.7 0.7 convolution_bitcast_fusion.5
  103.5 0.7 dynamic_update_slice.7
  105.2 0.7 convolution_bitcast_fusion.5
  107.0 0.7 dynamic_update_slice.7
  108.6 0.7 convolution_bitcast_fusion.5
  110.4 0.7 dynamic_update_slice.7
  111.3 20.0 %all_to_all.23 = bf16[16,16,4,256]{3,1,2,0:T(8,128)(2,1)S(1)} all-to-all(bf16[16,16,4,256]{3,1,2,0:T(8,128)(2,1)S(1)} %constant_dynamic-update-slice_fusion), channel_id=1, replica_groups=mesh['space'=32,'vel'=16] {'vel'}, dimensions={0} | all-to-all | bytes 1048576 | tf_op jit(solution)/shard_map/all_to_all | solution.py:18
  131.4 1.0 copy.29
  (233 shorter events, 36.4 us)
Async XLA Ops:
  0.0 19.9 %copy-start.2 = (bf16[5,16,16]{2,1,0:T(8,128)(2,1)S(1)}, bf16[5,16,16]{2,1,0:T(8,128)(2,1)}, u32[]{:S(2)}) copy-start(bf16[5,16,16]{2,1,0:T(8,128)(2,1)} %constant.108.clone) | copy-start | bytes 7684
  0.0 19.5 %copy-start.12 = (s32[16,6]{0,1:T(8,128)S(1)}, s32[16,6]{0,1:T(8,128)}, u32[]{:S(2)}) copy-start(s32[16,6]{0,1:T(8,128)} %param.19) | copy-start | bytes 1156
  0.0 19.7 %copy-start.13 = (s32[16,6]{0,1:T(8,128)S(1)}, s32[16,6]{0,1:T(8,128)}, u32[]{:S(2)}) copy-start(s32[16,6]{0,1:T(8,128)} %param.18) | copy-start | bytes 1156
  1.5 19.8 %copy-start.1 = (bf16[16,64,256]{2,1,0:T(8,128)(2,1)S(1)}, bf16[16,64,256]{2,1,0:T(8,128)(2,1)}, u32[]{:S(2)}) copy-start(bf16[16,64,256]{2,1,0:T(8,128)(2,1)} %param.15) | copy-start | bytes 1572868
  1.5 19.8 %copy-start.11 = (bf16[64,64,1]{1,0,2:T(8,128)(2,1)S(1)}, bf16[64,64,1]{1,0,2:T(8,128)(2,1)}, u32[]{:S(2)}) copy-start(bf16[64,64,1]{1,0,2:T(8,128)(2,1)} %constant.122) | copy-start | bytes 24580
  3.7 17.9 %copy-start.10 = (bf16[64,64,1]{1,0,2:T(8,128)(2,1)S(1)}, bf16[64,64,1]{1,0,2:T(8,128)(2,1)}, u32[]{:S(2)}) copy-start(bf16[64,64,1]{1,0,2:T(8,128)(2,1)} %constant.123) | copy-start | bytes 24580
  3.8 18.9 %collective-permute-start = (bf16[16,16,256]{2,1,0:T(8,128)(2,1)S(1)}, bf16[16,16,256]{2,1,0:T(8,128)(2,1)S(1)}, u32[]{:S(2)}, u32[]{:S(2)}) collective-permute-start(bf16[16,16,256]{2,1,0:T(8,128)(2,1)S(1)} %get-tuple-element.63), channel_id=1, source_target_pairs={{496,0},{0,16},{16,32},{32,48},{48,64},{64,80},{80,96},{96,112},{1... | collective-permute-start | bytes 393224 | tf_op jit(solution)/shard_map/ppermute | solution.py:25
  7.7 15.7 %collective-permute-start.1 = (bf16[16,16,256]{2,1,0:T(8,128)(2,1)S(1)}, bf16[16,16,256]{2,1,0:T(8,128)(2,1)}, u32[]{:S(2)}, u32[]{:S(2)}) collective-permute-start(bf16[16,16,256]{2,1,0:T(8,128)(2,1)S(1)} %get-tuple-element.64), channel_id=1, source_target_pairs={{16,0},{32,16},{48,32},{64,48},{80,64},{96,80},{112,96},{128,112},... | collective-permute-start | bytes 393224 | tf_op jit(solution)/shard_map/ppermute | solution.py:25
  21.6 0.7 copy-start.9
  22.7 3.3 %copy-start.3 = (bf16[96,16,16]{2,1,0:T(8,128)(2,1)S(1)}, bf16[96,16,16]{2,1,0:T(8,128)(2,1)}, u32[]{:S(2)}) copy-start(bf16[96,16,16]{2,1,0:T(8,128)(2,1)} %gather_fusion) | copy-start | bytes 147460
  22.7 0.6 copy-start.6
  27.5 0.8 copy-start.8
  29.5 9.2 %copy-start.5 = (f32[5,4096]{1,0:T(8,128)S(1)}, f32[5,4096]{1,0:T(8,128)}, u32[]{:S(2)}) copy-start(f32[5,4096]{1,0:T(8,128)} %param.21) | copy-start | bytes 245764
  29.5 9.2 %copy-start.7 = (f32[4,4096]{1,0:T(4,128)S(1)}, f32[4,4096]{1,0:T(4,128)}, u32[]{:S(2)}) copy-start(f32[4,4096]{1,0:T(4,128)} %param.20) | copy-start | bytes 196612
  29.6 26.6 %copy-start = (f32[256,256,1]{1,0,2:T(8,128)S(1)}, f32[256,256,1]{1,0,2:T(8,128)}, u32[]{:S(2)}) copy-start(f32[256,256,1]{1,0,2:T(8,128)} %constant.278) | copy-start | bytes 786436
  29.6 26.5 %copy-start.4 = (f32[16,16,1]{1,0,2:T(8,128)S(1)}, f32[16,16,1]{1,0,2:T(8,128)}, u32[]{:S(2)}) copy-start(f32[16,16,1]{1,0,2:T(8,128)} %constant.279) | copy-start | bytes 3076
  30.7 25.4 %all-to-all-start = ((bf16[16,64,256]{2,0,1:T(8,128)(2,1)}), bf16[16,64,256]{2,0,1:T(8,128)(2,1)S(1)}, u32[]{:S(2)}, u32[]{:S(2)}) async-start(bf16[16,64,256]{2,0,1:T(8,128)(2,1)} %copy.25), calls=%async_computation | async-start | bytes 1048576 | tf_op jit(solution)/shard_map/all_to_all | solution.py:190
